TPU v7x, 32 devices: a whole 2x2x4 slice. The times are simulated.
32 devices in a mesh: sub: 8 (over y, x, core), coarse: 4 (over z).
Axes of the slice: x: 2, y: 2, z: 4, core: 2. Of those that a mesh axis runs over, the one named last changes fastest.
Arguments:
- right_side: float32 [8, 4, 128, 128], P('sub', 'coarse'), may hold values from -150 to 150
- diagonal: float32 [8, 4, 128, 128], P('sub', 'coarse'), may hold values from 2 to 8
- cell_link: float32 [8, 4, 128, 128], P('sub', 'coarse'), may hold values from 0.2 to 0.9
- block_inverse: float32 [8, 4, 128, 128, 128], P('sub', 'coarse'), may hold values from -1 to 1
- coupling: float32 [8, 4, 4, 128, 128], P('sub', 'coarse'), may hold values from -0.26516503 to 0.26516503
- coarse_basis: float32 [8, 4, 128, 128], P('sub', 'coarse'), may hold values from -6 to 6
- coarse_inverse: float32 [512, 512], P('coarse'), may hold values from -0.25 to 0.25
- partner: int32 [8, 4], P('sub'), may hold values from 0 to 7, as said below
- margin_width: int32 [8, 4], P('sub'), may hold values from 4 to 8, as said below
- margin_blocks: int32 [8, 4, 4, 8], P('sub', 'coarse'), may hold values from 0 to 127
- aggregate: int32 [8, 4, 128], P('sub', 'coarse'), may hold values from 0 to 511, as said below
Outputs:
- solution: float32 [8, 4, 128, 128], P('sub', 'coarse')
Inputs may be any that keep to these rules, and one draw needn't show every extreme that they name: partner[s, r] differs from s, partner[partner[s, r], r] = s, and the 4 partners of one subdomain are distinct. margin_width[partner[s, r], r] = margin_width[s, r]; every colour round has a pair with width 8. `margin_blocks`: entries with w >= margin_width[s, r] are not used. aggregate[s, c, b] lies in (s * 4 + c) * 16 to (s * 4 + c + 1) * 16 - 1, and every one of these 16 aggregates has a block of part [s, c].
All inputs are finite; a program needn't handle non-finite values.
Results may differ from a plain program's by a relative error of at most 0.0003.
Values sent between devices are 32-bit elements; how exact they have to be, the bound alone decides.
No kernel may reach another device: no remote copies, remote signals or barrier semaphores. Data moves between devices by JAX's collectives and lax.ppermute only.
A program may use at most 64 MiB of HBM per device.

v0:
```python
import jax
import jax.numpy as jnp
from jax import lax
from jax.sharding import PartitionSpec as P

BS = 128
BPD = 128
AGG_DEV = 16
ITERS = 4


def givens_solve(columns, beta):
    steps_count = len(columns)
    cosines = []
    sines = []
    side_terms = [beta] + [jnp.zeros_like(beta) for unused in range(steps_count)]
    triangle = []
    for column_id in range(steps_count):
        column = list(columns[column_id])
        for row_id in range(column_id):
            upper = column[row_id]
            lower = column[row_id + 1]
            column[row_id] = cosines[row_id] * upper + sines[row_id] * lower
            column[row_id + 1] = cosines[row_id] * lower - sines[row_id] * upper
        upper = column[column_id]
        lower = column[column_id + 1]
        radius = jnp.sqrt(upper * upper + lower * lower)
        cosine = upper / radius
        sine_value = lower / radius
        column[column_id] = radius
        cosines.append(cosine)
        sines.append(sine_value)
        side_terms[column_id + 1] = -sine_value * side_terms[column_id]
        side_terms[column_id] = cosine * side_terms[column_id]
        triangle.append(column)
    weights = [None] * steps_count
    for column_id in reversed(range(steps_count)):
        running = side_terms[column_id]
        for later_col in range(column_id + 1, steps_count):
            running = running - triangle[later_col][column_id] * weights[later_col]
        weights[column_id] = running / triangle[column_id][column_id]
    return weights


def on_device(
    right_side,
    diagonal,
    cell_link,
    block_inverse,
    coupling,
    coarse_basis,
    coarse_inverse,
    partner,
    margin_width,
    margin_blocks,
    aggregate,
):
    highest = lax.Precision.HIGHEST
    block_count = right_side.shape[2]
    unknowns = right_side.shape[3]
    factor = (BS * BPD / AGG_DEV) ** (-0.5)
    inverse_blocks = block_inverse[0, 0]
    couplings = coupling[0, 0]
    basis_local = coarse_basis[0, 0]
    diagonal_local = diagonal[0, 0]
    link_local = cell_link[0, 0]
    paired = partner[0]
    widths = margin_width[0]
    blocks = margin_blocks[0, 0]
    member_of = aggregate[0, 0]
    aggregate_count = coarse_inverse.shape[1]
    member_table = (member_of[:, None] == jnp.arange(aggregate_count)[None, :]).astype(jnp.float32)
    rounds = blocks.shape[0]
    widest = blocks.shape[1]
    target = (blocks.reshape(-1)[:, None] == jnp.arange(block_count)[None, :]).astype(jnp.float32)
    live_mask = (jnp.arange(widest)[None, :] < widths[:, None]).astype(jnp.float32)

    def margin(values):
        outgoing = jnp.take(values, blocks.reshape(-1), axis=0).reshape(rounds, widest, unknowns)
        pieces = []
        for round_id in range(rounds):
            gathered = lax.all_gather(outgoing[round_id], "sub", axis=0, tiled=True)
            pieces.append(lax.dynamic_slice_in_dim(gathered, paired[round_id] * widest, widest, 0))
        incoming = jnp.stack(pieces)
        mapped = (
            jnp.einsum("rij,rwj->rwi", couplings, incoming, precision=highest)
            * live_mask[:, :, None]
        )
        return jnp.einsum(
            "kb,ki->bi", target, mapped.reshape(rounds * widest, unknowns), precision=highest
        )

    def squared_norm(values):
        return lax.psum(jnp.sum(values * values), ("sub", "coarse"))

    start_vector = right_side[0, 0]
    directions = []
    columns = []
    beta = jnp.sqrt(squared_norm(start_vector))
    basis_list = [start_vector / beta]
    for krylov_step in range(ITERS):
        current = basis_list[-1]
        inner = jnp.sum(basis_local * current, axis=1)
        restricted = lax.psum(
            jnp.dot(inner, member_table, precision=highest) * factor, ("sub", "coarse")
        )
        local_part = jnp.einsum(
            "bij,bj->bi", inverse_blocks, current + margin(current), precision=highest
        )
        coarse_part = jnp.dot(coarse_inverse, restricted, precision=highest)
        coarse_full = lax.all_gather(coarse_part, "coarse", axis=0, tiled=True)
        prolonged = jnp.dot(member_table, coarse_full, precision=highest)
        direction = local_part + prolonged[:, None] * basis_local
        directions.append(direction)
        flat_line = direction.reshape(-1)
        link_line = link_local.reshape(-1)
        zero_pad = jnp.zeros((1,), jnp.float32)
        ahead_terms = jnp.concatenate([flat_line[1:], zero_pad]) * link_line
        behind_terms = jnp.concatenate([zero_pad, (link_line * flat_line)[:-1]])
        product = (
            diagonal_local * direction
            - (ahead_terms + behind_terms).reshape(direction.shape)
            - margin(direction)
        )
        projected = lax.psum(
            jnp.stack([jnp.sum(vector * product) for vector in basis_list]), ("sub", "coarse")
        )
        for position in range(len(basis_list)):
            product = product - projected[position] * basis_list[position]
        norm_new = jnp.sqrt(squared_norm(product))
        columns.append([projected[position] for position in range(len(basis_list))] + [norm_new])
        basis_list.append(product / norm_new)
    weights = givens_solve(columns, beta)
    solution = weights[0] * directions[0]
    for position in range(1, ITERS):
        solution = solution + weights[position] * directions[position]
    return solution.reshape(right_side.shape)


def solution(mesh):
    placed = (
        P("sub", "coarse", None, None),
        P("sub", "coarse", None, None),
        P("sub", "coarse", None, None),
        P("sub", "coarse", None, None, None),
        P("sub", "coarse", None, None, None),
        P("sub", "coarse", None, None),
        P("coarse", None),
        P("sub", None),
        P("sub", None),
        P("sub", "coarse", None, None),
        P("sub", "coarse", None),
    )
    return jax.shard_map(
        on_device,
        mesh=mesh,
        in_specs=placed,
        out_specs=P("sub", "coarse", None, None),
        check_vma=False,
    )
```

profile of v0, /device:TPU:0, one launch (start us, length us, event | category | flops | bytes accessed | tf_op | source)
XLA Modules:
  0.0 958.9 jit_solution(15861982066872133460)
XLA Ops:
  0.9 1.5 multiply_reduce_fusion.14
  2.3 42.2 %psum.91 = f32[]{:T(128)} all-reduce(f32[]{:T(128)} %multiply_reduce_fusion.14), channel_id=1, replica_groups=mesh['sub'=8,'coarse'=4] {'sub','coarse'}, use_global_device_ids=true, to_apply=%region_1.0 | all-reduce | flops 1 | bytes 8 | tf_op jit(solution)/shard_map/psum | solution.py:94
  46.9 10.0 %all_gather.108 = f32[64,128]{1,0:T(8,128)S(1)} all-gather(f32[8,128]{1,0:T(8,128)S(1)} %get-tuple-element.63), channel_id=1, replica_groups=mesh['sub'=8,'coarse'=4] {'sub'}, dimensions={0}, use_global_device_ids=true | all-gather | bytes 36864 | tf_op jit(solution)/shard_map/all_gather | solution.py:82
  56.9 1.5 fusion.188
  59.0 8.1 all_gather.109
  67.9 9.1 all_gather.110
  77.6 8.1 all_gather.111
  87.8 15.4 %fusion.6 = f32[128,1,128]{2,1,0:T(1,128)S(1)} fusion(f32[128,128,1]{1,2,0:T(1,128)S(1)} %bitcast.355, f32[1,1,128,128,128]{4,3,2,1,0:T(8,128)} %param.16), kind=kOutput, calls=%fused_computation.14 | convolution fusion | flops 25165824 | bytes 8519680 | tf_op jit(solution)/shard_map/bij,bj->bi/dot_general | solution.py:107
  103.5 39.4 %psum.92 = f32[512]{0:T(512)S(1)} all-reduce(f32[512]{0:T(512)S(1)} %broadcast_multiply_fusion.3), channel_id=1, replica_groups=mesh['sub'=8,'coarse'=4] {'sub','coarse'}, use_global_device_ids=true, to_apply=%region_3.5 | all-reduce | flops 512 | bytes 4096 | tf_op jit(solution)/shard_map/psum | solution.py:104
  143.1 9.8 %all-gather = f32[4,1,128]{2,1,0:T(1,128)S(1)} all-gather(f32[1,1,128]{2,1,0:T(1,128)S(1)} %convolution_bitcast_fusion.7), channel_id=1, replica_groups=mesh['sub'=8,'coarse'=4] {'coarse'}, dimensions={0}, use_global_device_ids=true | all-gather | bytes 2560 | tf_op jit(solution)/shard_map/all_gather | solution.py:111
  153.9 9.8 %all_gather.113 = f32[64,128]{1,0:T(8,128)S(1)} all-gather(f32[8,128]{1,0:T(8,128)S(1)} %get-tuple-element.59), channel_id=1, replica_groups=mesh['sub'=8,'coarse'=4] {'sub'}, dimensions={0}, use_global_device_ids=true | all-gather | bytes 36864 | tf_op jit(solution)/shard_map/all_gather | solution.py:82
  163.8 9.1 all_gather.114
  172.8 8.1 all_gather.115
  180.9 9.1 all_gather.116
  191.5 37.8 %psum.93 = f32[]{:T(128)} all-reduce(f32[]{:T(128)} %get-tuple-element.80), channel_id=1, replica_groups=mesh['sub'=8,'coarse'=4] {'sub','coarse'}, use_global_device_ids=true, to_apply=%region_5.7 | all-reduce | flops 1 | bytes 8 | tf_op jit(solution)/shard_map/psum | solution.py:125
  229.3 1.3 multiply_reduce_fusion.12
  230.6 41.2 %psum.94 = f32[]{:T(128)} all-reduce(f32[]{:T(128)} %multiply_reduce_fusion.12), channel_id=1, replica_groups=mesh['sub'=8,'coarse'=4] {'sub','coarse'}, use_global_device_ids=true, to_apply=%region_7.9 | all-reduce | flops 1 | bytes 8 | tf_op jit(solution)/shard_map/psum | solution.py:94
  274.0 10.1 %all_gather.117 = f32[64,128]{1,0:T(8,128)S(1)} all-gather(f32[8,128]{1,0:T(8,128)S(1)} %get-tuple-element.55), channel_id=1, replica_groups=mesh['sub'=8,'coarse'=4] {'sub'}, dimensions={0}, use_global_device_ids=true | all-gather | bytes 36864 | tf_op jit(solution)/shard_map/all_gather | solution.py:82
  284.1 9.0 all_gather.118
  293.1 8.1 all_gather.119
  301.2 9.0 all_gather.120
  311.1 15.4 %fusion.4 = f32[128,1,128]{2,1,0:T(1,128)S(1)} fusion(f32[128,128,1]{1,2,0:T(1,128)S(1)} %bitcast.356, f32[1,1,128,128,128]{4,3,2,1,0:T(8,128)} %param.16), kind=kOutput, calls=%fused_computation.12 | convolution fusion | flops 25165824 | bytes 8519680 | tf_op jit(solution)/shard_map/bij,bj->bi/dot_general | solution.py:107
  326.8 37.7 %psum.95 = f32[512]{0:T(512)S(1)} all-reduce(f32[512]{0:T(512)S(1)} %broadcast_multiply_fusion.2), channel_id=1, replica_groups=mesh['sub'=8,'coarse'=4] {'sub','coarse'}, use_global_device_ids=true, to_apply=%region_9.11 | all-reduce | flops 512 | bytes 4096 | tf_op jit(solution)/shard_map/psum | solution.py:104
  364.7 9.6 %all-gather.1 = f32[4,1,128]{2,1,0:T(1,128)S(1)} all-gather(f32[1,1,128]{2,1,0:T(1,128)S(1)} %convolution_bitcast_fusion.5), channel_id=1, replica_groups=mesh['sub'=8,'coarse'=4] {'coarse'}, dimensions={0}, use_global_device_ids=true | all-gather | bytes 2560 | tf_op jit(solution)/shard_map/all_gather | solution.py:111
  375.4 9.8 %all_gather.122 = f32[64,128]{1,0:T(8,128)S(1)} all-gather(f32[8,128]{1,0:T(8,128)S(1)} %get-tuple-element.51), channel_id=1, replica_groups=mesh['sub'=8,'coarse'=4] {'sub'}, dimensions={0}, use_global_device_ids=true | all-gather | bytes 36864 | tf_op jit(solution)/shard_map/all_gather | solution.py:82
  385.2 8.1 all_gather.123
  393.3 9.0 all_gather.124
  402.3 8.3 all_gather.125
  411.2 1.0 multiply_reduce_fusion.11
  412.2 1.3 pad_maximum_fusion.8
  413.5 37.6 %psum.96 = f32[2]{0:T(128)S(1)} all-reduce(f32[2]{0:T(128)S(1)} %pad_maximum_fusion.8), channel_id=1, replica_groups=mesh['sub'=8,'coarse'=4] {'sub','coarse'}, use_global_device_ids=true, to_apply=%region_12.14 | all-reduce | flops 2 | bytes 16 | tf_op jit(solution)/shard_map/psum | solution.py:125
  451.8 1.9 multiply_reduce_fusion.9
  453.6 41.7 %psum.97 = f32[]{:T(128)} all-reduce(f32[]{:T(128)} %get-tuple-element.21), channel_id=1, replica_groups=mesh['sub'=8,'coarse'=4] {'sub','coarse'}, use_global_device_ids=true, to_apply=%region_14.16 | all-reduce | flops 1 | bytes 8 | tf_op jit(solution)/shard_map/psum | solution.py:94
  496.8 10.1 %all_gather.126 = f32[64,128]{1,0:T(8,128)S(1)} all-gather(f32[8,128]{1,0:T(8,128)S(1)} %get-tuple-element.47), channel_id=1, replica_groups=mesh['sub'=8,'coarse'=4] {'sub'}, dimensions={0}, use_global_device_ids=true | all-gather | bytes 36864 | tf_op jit(solution)/shard_map/all_gather | solution.py:82
  506.9 8.1 all_gather.127
  515.0 9.0 all_gather.128
  524.0 8.1 all_gather.129
  533.0 15.4 %fusion.2 = f32[128,1,128]{2,1,0:T(1,128)S(1)} fusion(f32[128,128,1]{1,2,0:T(1,128)S(1)} %bitcast.357, f32[1,1,128,128,128]{4,3,2,1,0:T(8,128)} %param.16), kind=kOutput, calls=%fused_computation.10 | convolution fusion | flops 25165824 | bytes 8519680 | tf_op jit(solution)/shard_map/bij,bj->bi/dot_general | solution.py:107
  548.6 37.7 %psum.98 = f32[512]{0:T(512)S(1)} all-reduce(f32[512]{0:T(512)S(1)} %broadcast_multiply_fusion.1), channel_id=1, replica_groups=mesh['sub'=8,'coarse'=4] {'sub','coarse'}, use_global_device_ids=true, to_apply=%region_16.18 | all-reduce | flops 512 | bytes 4096 | tf_op jit(solution)/shard_map/psum | solution.py:104
  586.5 9.6 %all-gather.2 = f32[4,1,128]{2,1,0:T(1,128)S(1)} all-gather(f32[1,1,128]{2,1,0:T(1,128)S(1)} %convolution_bitcast_fusion.3), channel_id=1, replica_groups=mesh['sub'=8,'coarse'=4] {'coarse'}, dimensions={0}, use_global_device_ids=true | all-gather | bytes 2560 | tf_op jit(solution)/shard_map/all_gather | solution.py:111
  597.2 9.8 %all_gather.131 = f32[64,128]{1,0:T(8,128)S(1)} all-gather(f32[8,128]{1,0:T(8,128)S(1)} %get-tuple-element.43), channel_id=1, replica_groups=mesh['sub'=8,'coarse'=4] {'sub'}, dimensions={0}, use_global_device_ids=true | all-gather | bytes 36864 | tf_op jit(solution)/shard_map/all_gather | solution.py:82
  607.0 9.0 all_gather.132
  616.1 8.5 all_gather.133
  624.6 9.0 all_gather.134
  635.2 1.9 pad_maximum_fusion.9
  637.2 37.6 %psum.99 = f32[3]{0:T(128)S(1)} all-reduce(f32[3]{0:T(128)S(1)} %pad_maximum_fusion.9), channel_id=1, replica_groups=mesh['sub'=8,'coarse'=4] {'sub','coarse'}, use_global_device_ids=true, to_apply=%region_20.22 | all-reduce | flops 3 | bytes 24 | tf_op jit(solution)/shard_map/psum | solution.py:125
  675.4 2.5 multiply_reduce_fusion.5
  677.9 40.7 %psum.100 = f32[]{:T(128)} all-reduce(f32[]{:T(128)} %get-tuple-element.17), channel_id=1, replica_groups=mesh['sub'=8,'coarse'=4] {'sub','coarse'}, use_global_device_ids=true, to_apply=%region_22.24 | all-reduce | flops 1 | bytes 8 | tf_op jit(solution)/shard_map/psum | solution.py:94
  720.0 10.0 %all_gather.135 = f32[64,128]{1,0:T(8,128)S(1)} all-gather(f32[8,128]{1,0:T(8,128)S(1)} %get-tuple-element.39), channel_id=1, replica_groups=mesh['sub'=8,'coarse'=4] {'sub'}, dimensions={0}, use_global_device_ids=true | all-gather | bytes 36864 | tf_op jit(solution)/shard_map/all_gather | solution.py:82
  730.0 9.0 all_gather.136
  739.1 8.1 all_gather.137
  747.1 9.0 all_gather.138
  757.1 15.4 %fusion = f32[128,1,128]{2,1,0:T(1,128)S(1)} fusion(f32[128,128,1]{1,2,0:T(1,128)S(1)} %bitcast.358, f32[1,1,128,128,128]{4,3,2,1,0:T(8,128)} %param.16), kind=kOutput, calls=%fused_computation.8 | convolution fusion | flops 25165824 | bytes 8519680 | tf_op jit(solution)/shard_map/bij,bj->bi/dot_general | solution.py:107
  772.7 37.7 %psum.101 = f32[512]{0:T(512)S(1)} all-reduce(f32[512]{0:T(512)S(1)} %broadcast_multiply_fusion), channel_id=1, replica_groups=mesh['sub'=8,'coarse'=4] {'sub','coarse'}, use_global_device_ids=true, to_apply=%region_24.26 | all-reduce | flops 512 | bytes 4096 | tf_op jit(solution)/shard_map/psum | solution.py:104
  810.6 9.6 %all-gather.3 = f32[4,1,128]{2,1,0:T(1,128)S(1)} all-gather(f32[1,1,128]{2,1,0:T(1,128)S(1)} %convolution_bitcast_fusion.1), channel_id=1, replica_groups=mesh['sub'=8,'coarse'=4] {'coarse'}, dimensions={0}, use_global_device_ids=true | all-gather | bytes 2560 | tf_op jit(solution)/shard_map/all_gather | solution.py:111
  821.3 9.8 %all_gather.140 = f32[64,128]{1,0:T(8,128)S(1)} all-gather(f32[8,128]{1,0:T(8,128)S(1)} %get-tuple-element.35), channel_id=1, replica_groups=mesh['sub'=8,'coarse'=4] {'sub'}, dimensions={0}, use_global_device_ids=true | all-gather | bytes 36864 | tf_op jit(solution)/shard_map/all_gather | solution.py:82
  831.1 8.2 all_gather.141
  839.4 9.0 all_gather.142
  848.4 8.1 all_gather.143
  857.1 1.0 multiply_reduce_fusion.4
  858.1 2.5 pad_maximum_fusion.10
  860.6 37.6 %psum.102 = f32[4]{0:T(128)S(1)} all-reduce(f32[4]{0:T(128)S(1)} %pad_maximum_fusion.10), channel_id=1, replica_groups=mesh['sub'=8,'coarse'=4] {'sub','coarse'}, use_global_device_ids=true, to_apply=%region_29.31 | all-reduce | flops 4 | bytes 32 | tf_op jit(solution)/shard_map/psum | solution.py:125
  905.5 3.0 multiply_reduce_fusion
  908.5 41.8 %psum.103 = f32[]{:T(128)} all-reduce(f32[]{:T(128)} %multiply_reduce_fusion), channel_id=1, replica_groups=mesh['sub'=8,'coarse'=4] {'sub','coarse'}, use_global_device_ids=true, to_apply=%region_31.33 | all-reduce | flops 1 | bytes 8 | tf_op jit(solution)/shard_map/psum | solution.py:94
  (119 shorter events, 22.8 us)
Async XLA Ops:
  0.0 87.0 %copy-start = (f32[1,1,4,128,128]{4,3,2,1,0:T(8,128)S(1)}, f32[1,1,4,128,128]{4,3,2,1,0:T(8,128)}, u32[]{:S(2)}) copy-start(f32[1,1,4,128,128]{4,3,2,1,0:T(8,128)} %param.17) | copy-start | bytes 786436
  0.0 153.1 %copy-start.1 = (f32[1,1,128,128]{3,2,1,0:T(8,128)S(1)}, f32[1,1,128,128]{3,2,1,0:T(8,128)}, u32[]{:S(2)}) copy-start(f32[1,1,128,128]{3,2,1,0:T(8,128)} %param.18) | copy-start | bytes 196612
  0.0 103.2 %copy-start.5 = (s32[1,1,128]{2,1,0:T(1,128)S(1)}, s32[1,1,128]{2,1,0:T(1,128)}, u32[]{:S(2)}) copy-start(s32[1,1,128]{2,1,0:T(1,128)} %param.23) | copy-start | bytes 1540
  0.0 142.9 %copy-start.2 = (f32[128,512]{1,0:T(8,128)S(1)}, f32[128,512]{1,0:T(8,128)}, u32[]{:S(2)}) copy-start(f32[128,512]{1,0:T(8,128)} %param.19) | copy-start | bytes 786436
  0.0 190.4 %copy-start.3 = (f32[1,1,128,128]{3,2,1,0:T(8,128)S(1)}, f32[1,1,128,128]{3,2,1,0:T(8,128)}, u32[]{:S(2)}) copy-start(f32[1,1,128,128]{3,2,1,0:T(8,128)} %param.15) | copy-start | bytes 196612
  0.0 190.5 %copy-start.4 = (f32[1,1,128,128]{3,2,1,0:T(8,128)S(1)}, f32[1,1,128,128]{3,2,1,0:T(8,128)}, u32[]{:S(2)}) copy-start(f32[1,1,128,128]{3,2,1,0:T(8,128)} %param.14) | copy-start | bytes 196612
where the time goes:
time: 971 us; the launch traced here: 959 us
  blocking collectives  835 us (86%)
  matrix products  73.9 us (8%)
  other arithmetic  21.1 us (2%)
  between operations  20.1 us (2%)
    all_gather x32, blocking collectives, margin(): gathered = lax.all_gather(outgoing[round_id], 'sub', axis=0, tiled=True)  286 us
    psum x5, blocking collectives, squared_norm(): return lax.psum(jnp.sum(values * values), ('sub', 'coarse'))  208 us
    psum x4, blocking collectives, on_device(): lax.psum(jnp.dot(inner, member_table, precision=highest) * factor, ('sub'...  152 us
    psum x4, blocking collectives, on_device(): lax.psum(jnp.stack([jnp.sum(vector * product) for vector in basis_list]),...  151 us
    dot_general x4, matrix products, on_device(): jnp.einsum('bij,bj->bi', inverse_blocks, current + margin(current), preci...  61.5 us
    all_gather x4, blocking collectives, on_device(): coarse_full = lax.all_gather(coarse_part, 'coarse', axis=0, tiled=True)  38.7 us

commit v1 on v0

--- a/solution.py
+++ b/solution.py
@@ -7,6 +7,23 @@
 BPD = 128
 AGG_DEV = 16
 ITERS = 4
+
+
+def laid_out(tiles, dim):
+    dims = list(tiles.shape[1:])
+    dims[dim] *= tiles.shape[0]
+    return jnp.moveaxis(tiles, 0, dim).reshape(dims)
+
+
+def collected_by_bits(array, axis):
+    size, index = (lax.axis_size(axis), lax.axis_index(axis))
+    blocks, apart = (array[None], 1)
+    while apart < size:
+        other = lax.ppermute(blocks, axis, [(i, i ^ apart) for i in range(size)])
+        low = index & apart == 0
+        blocks = jnp.concatenate([jnp.where(low, blocks, other), jnp.where(low, other, blocks)])
+        apart *= 2
+    return blocks
 
 
 def givens_solve(columns, beta):
@@ -79,7 +96,7 @@
         outgoing = jnp.take(values, blocks.reshape(-1), axis=0).reshape(rounds, widest, unknowns)
         pieces = []
         for round_id in range(rounds):
-            gathered = lax.all_gather(outgoing[round_id], "sub", axis=0, tiled=True)
+            gathered = laid_out(collected_by_bits(outgoing[round_id], "sub"), 0)
             pieces.append(lax.dynamic_slice_in_dim(gathered, paired[round_id] * widest, widest, 0))
         incoming = jnp.stack(pieces)
         mapped = (

time: 971 us -> 801 us (0.82)
  blocking collectives: 835 us -> 556 us
  starting transfers between devices: 0 us -> 78.7 us
  waiting for transfers between devices: 0 us -> 25.6 us
    all_gather x32 -> x0, blocking collectives: 286 us -> none  [margin(): gathered = lax.all_gather(outgoing[round_id], 'sub', axis=0, tiled=True)]
    ppermute x0 -> x96, starting transfers between devices: none -> 78.7 us  [collected_by_bits(): other = lax.ppermute(blocks, axis, [(i, i ^ apart) for i in range(size)])]
    ppermute x0 -> x96, waiting for transfers between devices: none -> 25.6 us  [collected_by_bits(): other = lax.ppermute(blocks, axis, [(i, i ^ apart) for i in range(size)])]
  transfers between devices with their start and end apart: 0 -> 96, of which waited for: 0 -> 39; matrix products, arithmetic and copies ran while one was open for 0% -> 1% of each run, Pallas kernels for 0% -> 0%
where the time goes in v1:
time: 801 us; the launch traced here: 790 us
  blocking collectives  556 us (69%)
  starting transfers between devices  78.7 us (10%)
  matrix products  76.2 us (10%)
  waiting for transfers between devices  25.6 us (3%)
  other arithmetic  22.1 us (3%)
  between operations  21.6 us (3%)
  local copies, waits for them, and re-layouts  9.33 us (1%)
    psum x5, blocking collectives, squared_norm(): return lax.psum(jnp.sum(values * values), ('sub', 'coarse'))  208 us
    psum x4, blocking collectives, on_device(): lax.psum(jnp.dot(inner, member_table, precision=highest) * factor, ('sub'...  157 us
    psum x4, blocking collectives, on_device(): lax.psum(jnp.stack([jnp.sum(vector * product) for vector in basis_list]),...  152 us
    ppermute x96, starting transfers between devices, collected_by_bits(): other = lax.ppermute(blocks, axis, [(i, i ^ apart) for i in range(size)])  78.7 us
    dot_general x4, matrix products, on_device(): jnp.einsum('bij,bj->bi', inverse_blocks, current + margin(current), preci...  61.5 us
    all_gather x4, blocking collectives, on_device(): coarse_full = lax.all_gather(coarse_part, 'coarse', axis=0, tiled=True)  38.7 us
    ppermute x96, waiting for transfers between devices, collected_by_bits(): other = lax.ppermute(blocks, axis, [(i, i ^ apart) for i in range(size)])  25.6 us
  transfers between devices with their start and end apart: 96, of which 39 were waited for; matrix products, arithmetic and copies ran while one was open for 1% of the time, Pallas kernels for 0%

profile of v1, /device:TPU:0, one launch (start us, length us, event | category | flops | bytes accessed | tf_op | source)
XLA Modules:
  0.0 790.0 jit_solution(880800471064364964)
XLA Ops:
  0.9 1.5 multiply_reduce_fusion.14
  2.3 42.2 %psum.91 = f32[]{:T(128)} all-reduce(f32[]{:T(128)} %multiply_reduce_fusion.14), channel_id=1, replica_groups=mesh['sub'=8,'coarse'=4] {'sub','coarse'}, use_global_device_ids=true, to_apply=%region_1.0 | all-reduce | flops 1 | bytes 8 | tf_op jit(solution)/shard_map/psum | solution.py:111
  49.6 40.3 %psum.92 = f32[512]{0:T(512)S(1)} all-reduce(f32[512]{0:T(512)S(1)} %broadcast_multiply_fusion.3), channel_id=1, replica_groups=mesh['sub'=8,'coarse'=4] {'sub','coarse'}, use_global_device_ids=true, to_apply=%region_3.5 | all-reduce | flops 512 | bytes 4096 | tf_op jit(solution)/shard_map/psum | solution.py:121
  89.9 1.2 convolution_bitcast_fusion.7
  91.1 9.8 %all-gather = f32[4,1,128]{2,1,0:T(1,128)S(1)} all-gather(f32[1,1,128]{2,1,0:T(1,128)S(1)} %convolution_bitcast_fusion.7), channel_id=1, replica_groups=mesh['sub'=8,'coarse'=4] {'coarse'}, dimensions={0}, use_global_device_ids=true | all-gather | bytes 2560 | tf_op jit(solution)/shard_map/all_gather | solution.py:128
  101.8 1.5 fusion.180
  105.9 2.3 collective-permute-start.1
  108.3 1.9 collective-permute-start.7
  110.3 1.5 collective-permute-done.4
  111.9 1.6 collective-permute-start.2
  114.0 1.6 collective-permute-start.8
  117.8 1.5 collective-permute-done.11
  120.2 15.4 %fusion.6 = f32[128,1,128]{2,1,0:T(1,128)S(1)} fusion(f32[128,128,1]{1,2,0:T(1,128)S(1)} %bitcast.611, f32[1,1,128,128,128]{4,3,2,1,0:T(8,128)} %param.16), kind=kOutput, calls=%fused_computation.14 | convolution fusion | flops 25165824 | bytes 8519680 | tf_op jit(solution)/shard_map/bij,bj->bi/dot_general | solution.py:124
  138.8 1.5 collective-permute-start.16
  140.8 1.5 collective-permute-start.22
  143.0 1.6 collective-permute-start.17
  145.1 1.6 collective-permute-start.23
  146.8 1.5 collective-permute-done.20
  150.4 37.8 %psum.93 = f32[]{:T(128)} all-reduce(f32[]{:T(128)} %get-tuple-element.320), channel_id=1, replica_groups=mesh['sub'=8,'coarse'=4] {'sub','coarse'}, use_global_device_ids=true, to_apply=%region_5.7 | all-reduce | flops 1 | bytes 8 | tf_op jit(solution)/shard_map/psum | solution.py:142
  188.2 1.3 multiply_reduce_fusion.12
  189.5 42.5 %psum.94 = f32[]{:T(128)} all-reduce(f32[]{:T(128)} %multiply_reduce_fusion.12), channel_id=1, replica_groups=mesh['sub'=8,'coarse'=4] {'sub','coarse'}, use_global_device_ids=true, to_apply=%region_7.9 | all-reduce | flops 1 | bytes 8 | tf_op jit(solution)/shard_map/psum | solution.py:111
  235.4 38.7 %psum.95 = f32[512]{0:T(512)S(1)} all-reduce(f32[512]{0:T(512)S(1)} %broadcast_multiply_fusion.2), channel_id=1, replica_groups=mesh['sub'=8,'coarse'=4] {'sub','coarse'}, use_global_device_ids=true, to_apply=%region_9.11 | all-reduce | flops 512 | bytes 4096 | tf_op jit(solution)/shard_map/psum | solution.py:121
  274.4 9.6 %all-gather.1 = f32[4,1,128]{2,1,0:T(1,128)S(1)} all-gather(f32[1,1,128]{2,1,0:T(1,128)S(1)} %convolution_bitcast_fusion.5), channel_id=1, replica_groups=mesh['sub'=8,'coarse'=4] {'coarse'}, dimensions={0}, use_global_device_ids=true | all-gather | bytes 2560 | tf_op jit(solution)/shard_map/all_gather | solution.py:128
  286.4 2.3 collective-permute-start.25
  288.9 1.9 collective-permute-start.31
  290.9 2.0 collective-permute-start.26
  299.8 15.4 %fusion.4 = f32[128,1,128]{2,1,0:T(1,128)S(1)} fusion(f32[128,128,1]{1,2,0:T(1,128)S(1)} %bitcast.612, f32[1,1,128,128,128]{4,3,2,1,0:T(8,128)} %param.16), kind=kOutput, calls=%fused_computation.12 | convolution fusion | flops 25165824 | bytes 8519680 | tf_op jit(solution)/shard_map/bij,bj->bi/dot_general | solution.py:124
  317.8 1.6 collective-permute-start.37
  319.9 1.5 collective-permute-start.43
  330.6 1.4 pad_maximum_fusion.72
  332.0 38.1 %psum.96 = f32[2]{0:T(128)S(1)} all-reduce(f32[2]{0:T(128)S(1)} %pad_maximum_fusion.72), channel_id=1, replica_groups=mesh['sub'=8,'coarse'=4] {'sub','coarse'}, use_global_device_ids=true, to_apply=%region_12.14 | all-reduce | flops 2 | bytes 16 | tf_op jit(solution)/shard_map/psum | solution.py:142
  370.7 1.9 multiply_reduce_fusion.9
  372.6 40.9 %psum.97 = f32[]{:T(128)} all-reduce(f32[]{:T(128)} %get-tuple-element.21), channel_id=1, replica_groups=mesh['sub'=8,'coarse'=4] {'sub','coarse'}, use_global_device_ids=true, to_apply=%region_14.16 | all-reduce | flops 1 | bytes 8 | tf_op jit(solution)/shard_map/psum | solution.py:111
  416.3 39.7 %psum.98 = f32[512]{0:T(512)S(1)} all-reduce(f32[512]{0:T(512)S(1)} %broadcast_multiply_fusion.1), channel_id=1, replica_groups=mesh['sub'=8,'coarse'=4] {'sub','coarse'}, use_global_device_ids=true, to_apply=%region_16.18 | all-reduce | flops 512 | bytes 4096 | tf_op jit(solution)/shard_map/psum | solution.py:121
  456.3 9.7 %all-gather.2 = f32[4,1,128]{2,1,0:T(1,128)S(1)} all-gather(f32[1,1,128]{2,1,0:T(1,128)S(1)} %convolution_bitcast_fusion.3), channel_id=1, replica_groups=mesh['sub'=8,'coarse'=4] {'coarse'}, dimensions={0}, use_global_device_ids=true | all-gather | bytes 2560 | tf_op jit(solution)/shard_map/all_gather | solution.py:128
  469.0 2.3 collective-permute-start.49
  471.4 1.9 collective-permute-start.55
  473.5 2.0 collective-permute-start.50
  475.7 2.0 collective-permute-start.56
  477.9 1.4 collective-permute-done.53
  479.5 2.0 collective-permute-done.59
  482.4 15.4 %fusion.2 = f32[128,1,128]{2,1,0:T(1,128)S(1)} fusion(f32[128,128,1]{1,2,0:T(1,128)S(1)} %bitcast.613, f32[1,1,128,128,128]{4,3,2,1,0:T(8,128)} %param.16), kind=kOutput, calls=%fused_computation.10 | convolution fusion | flops 25165824 | bytes 8519680 | tf_op jit(solution)/shard_map/bij,bj->bi/dot_general | solution.py:124
  501.0 1.5 collective-permute-start.64
  503.0 1.5 collective-permute-start.70
  504.7 2.0 collective-permute-start.65
  506.9 2.0 collective-permute-start.71
  509.0 1.5 collective-permute-done.68
  512.3 2.0 pad_maximum_fusion.73
  514.3 38.0 %psum.99 = f32[3]{0:T(128)S(1)} all-reduce(f32[3]{0:T(128)S(1)} %pad_maximum_fusion.73), channel_id=1, replica_groups=mesh['sub'=8,'coarse'=4] {'sub','coarse'}, use_global_device_ids=true, to_apply=%region_20.22 | all-reduce | flops 3 | bytes 24 | tf_op jit(solution)/shard_map/psum | solution.py:142
  552.9 2.6 multiply_reduce_fusion.5
  555.5 42.0 %psum.100 = f32[]{:T(128)} all-reduce(f32[]{:T(128)} %get-tuple-element.17), channel_id=1, replica_groups=mesh['sub'=8,'coarse'=4] {'sub','coarse'}, use_global_device_ids=true, to_apply=%region_22.24 | all-reduce | flops 1 | bytes 8 | tf_op jit(solution)/shard_map/psum | solution.py:111
  600.3 38.7 %psum.101 = f32[512]{0:T(512)S(1)} all-reduce(f32[512]{0:T(512)S(1)} %broadcast_multiply_fusion), channel_id=1, replica_groups=mesh['sub'=8,'coarse'=4] {'sub','coarse'}, use_global_device_ids=true, to_apply=%region_24.26 | all-reduce | flops 512 | bytes 4096 | tf_op jit(solution)/shard_map/psum | solution.py:121
  639.3 9.6 %all-gather.3 = f32[4,1,128]{2,1,0:T(1,128)S(1)} all-gather(f32[1,1,128]{2,1,0:T(1,128)S(1)} %convolution_bitcast_fusion.1), channel_id=1, replica_groups=mesh['sub'=8,'coarse'=4] {'coarse'}, dimensions={0}, use_global_device_ids=true | all-gather | bytes 2560 | tf_op jit(solution)/shard_map/all_gather | solution.py:128
  653.2 2.3 collective-permute-start.73
  655.7 1.9 collective-permute-start.79
  657.7 2.0 collective-permute-start.74
  666.6 15.4 %fusion = f32[128,1,128]{2,1,0:T(1,128)S(1)} fusion(f32[128,128,1]{1,2,0:T(1,128)S(1)} %bitcast.614, f32[1,1,128,128,128]{4,3,2,1,0:T(8,128)} %param.16), kind=kOutput, calls=%fused_computation.8 | convolution fusion | flops 25165824 | bytes 8519680 | tf_op jit(solution)/shard_map/bij,bj->bi/dot_general | solution.py:124
  684.6 1.6 collective-permute-start.85
  686.7 1.5 collective-permute-start.91
  690.9 1.1 collective-permute-start.92
  697.4 2.7 pad_maximum_fusion.74
  700.1 38.1 %psum.102 = f32[4]{0:T(128)S(1)} all-reduce(f32[4]{0:T(128)S(1)} %pad_maximum_fusion.74), channel_id=1, replica_groups=mesh['sub'=8,'coarse'=4] {'sub','coarse'}, use_global_device_ids=true, to_apply=%region_29.31 | all-reduce | flops 4 | bytes 32 | tf_op jit(solution)/shard_map/psum | solution.py:142
  744.0 3.3 multiply_reduce_fusion
  747.3 40.8 %psum.103 = f32[]{:T(128)} all-reduce(f32[]{:T(128)} %multiply_reduce_fusion), channel_id=1, replica_groups=mesh['sub'=8,'coarse'=4] {'sub','coarse'}, use_global_device_ids=true, to_apply=%region_31.33 | all-reduce | flops 1 | bytes 8 | tf_op jit(solution)/shard_map/psum | solution.py:111
  (445 shorter events, 72.8 us)
Async XLA Ops:
  46.9 58.9 %collective-permute-start = (f32[1,8,128]{2,1,0:T(8,128)S(1)}, f32[1,8,128]{2,1,0:T(8,128)S(1)}, u32[]{:S(2)}, u32[]{:S(2)}) collective-permute-start(f32[1,8,128]{2,1,0:T(8,128)S(1)} %get-tuple-element.297), channel_id=1, source_target_pairs={{0,4},{4,0},{8,12},{12,8},{16,20},{20,16},{24,28},{28,24},{1,5},{5... | collective-permute-start | bytes 12296 | tf_op jit(solution)/shard_map/ppermute | solution.py:22
  46.9 58.9 %collective-permute-start.3 = (f32[1,8,128]{2,1,0:T(8,128)S(1)}, f32[1,8,128]{2,1,0:T(8,128)S(1)}, u32[]{:S(2)}, u32[]{:S(2)}) collective-permute-start(f32[1,8,128]{2,1,0:T(8,128)S(1)} %get-tuple-element.300), channel_id=1, source_target_pairs={{0,4},{4,0},{8,12},{12,8},{16,20},{20,16},{24,28},{28,24},{1,5},{5... | collective-permute-start | bytes 12296 | tf_op jit(solution)/shard_map/ppermute | solution.py:22
  47.4 58.4 %collective-permute-start.6 = (f32[1,8,128]{2,1,0:T(8,128)S(1)}, f32[1,8,128]{2,1,0:T(8,128)S(1)}, u32[]{:S(2)}, u32[]{:S(2)}) collective-permute-start(f32[1,8,128]{2,1,0:T(8,128)S(1)} %get-tuple-element.299), channel_id=1, source_target_pairs={{0,4},{4,0},{8,12},{12,8},{16,20},{20,16},{24,28},{28,24},{1,5},{5... | collective-permute-start | bytes 12296 | tf_op jit(solution)/shard_map/ppermute | solution.py:22
  47.5 58.3 %collective-permute-start.9 = (f32[1,8,128]{2,1,0:T(8,128)S(1)}, f32[1,8,128]{2,1,0:T(8,128)S(1)}, u32[]{:S(2)}, u32[]{:S(2)}) collective-permute-start(f32[1,8,128]{2,1,0:T(8,128)S(1)} %get-tuple-element.298), channel_id=1, source_target_pairs={{0,4},{4,0},{8,12},{12,8},{16,20},{20,16},{24,28},{28,24},{1,5},{5... | collective-permute-start | bytes 12296 | tf_op jit(solution)/shard_map/ppermute | solution.py:22
  105.9 4.5 collective-permute-start.1
  108.3 5.7 collective-permute-start.7
  111.9 4.2 collective-permute-start.2
  114.0 3.8 collective-permute-start.8
  138.2 4.1 collective-permute-start.13
  138.8 4.1 collective-permute-start.16
  140.3 4.2 collective-permute-start.19
  140.8 4.3 collective-permute-start.22
  142.4 4.4 collective-permute-start.14
  143.0 3.8 collective-permute-start.17
  144.5 3.8 collective-permute-start.20
  145.1 3.8 collective-permute-start.23
  234.1 52.2 %collective-permute-start.24 = (f32[1,8,128]{2,1,0:T(8,128)S(1)}, f32[1,8,128]{2,1,0:T(8,128)S(1)}, u32[]{:S(2)}, u32[]{:S(2)}) collective-permute-start(f32[1,8,128]{2,1,0:T(8,128)S(1)} %get-tuple-element.261), channel_id=1, source_target_pairs={{0,4},{4,0},{8,12},{12,8},{16,20},{20,16},{24,28},{28,24},{1,5},{5... | collective-permute-start | bytes 12296 | tf_op jit(solution)/shard_map/ppermute | solution.py:22
  234.2 52.2 %collective-permute-start.27 = (f32[1,8,128]{2,1,0:T(8,128)S(1)}, f32[1,8,128]{2,1,0:T(8,128)S(1)}, u32[]{:S(2)}, u32[]{:S(2)}) collective-permute-start(f32[1,8,128]{2,1,0:T(8,128)S(1)} %get-tuple-element.264), channel_id=1, source_target_pairs={{0,4},{4,0},{8,12},{12,8},{16,20},{20,16},{24,28},{28,24},{1,5},{5... | collective-permute-start | bytes 12296 | tf_op jit(solution)/shard_map/ppermute | solution.py:22
  234.7 51.7 %collective-permute-start.30 = (f32[1,8,128]{2,1,0:T(8,128)S(1)}, f32[1,8,128]{2,1,0:T(8,128)S(1)}, u32[]{:S(2)}, u32[]{:S(2)}) collective-permute-start(f32[1,8,128]{2,1,0:T(8,128)S(1)} %get-tuple-element.263), channel_id=1, source_target_pairs={{0,4},{4,0},{8,12},{12,8},{16,20},{20,16},{24,28},{28,24},{1,5},{5... | collective-permute-start | bytes 12296 | tf_op jit(solution)/shard_map/ppermute | solution.py:22
  234.7 51.7 %collective-permute-start.33 = (f32[1,8,128]{2,1,0:T(8,128)S(1)}, f32[1,8,128]{2,1,0:T(8,128)S(1)}, u32[]{:S(2)}, u32[]{:S(2)}) collective-permute-start(f32[1,8,128]{2,1,0:T(8,128)S(1)} %get-tuple-element.262), channel_id=1, source_target_pairs={{0,4},{4,0},{8,12},{12,8},{16,20},{20,16},{24,28},{28,24},{1,5},{5... | collective-permute-start | bytes 12296 | tf_op jit(solution)/shard_map/ppermute | solution.py:22
  286.4 4.5 collective-permute-start.25
  288.8 4.1 collective-permute-start.28
  288.9 5.1 collective-permute-start.31
  290.8 4.3 collective-permute-start.34
  290.9 5.3 collective-permute-start.26
  292.9 3.8 collective-permute-start.29
  294.0 3.8 collective-permute-start.32
  295.1 3.8 collective-permute-start.35
  317.8 4.1 collective-permute-start.37
  319.9 4.2 collective-permute-start.43
  322.0 4.4 collective-permute-start.38
  324.1 3.8 collective-permute-start.44
  415.0 53.9 %collective-permute-start.48 = (f32[1,8,128]{2,1,0:T(8,128)S(1)}, f32[1,8,128]{2,1,0:T(8,128)S(1)}, u32[]{:S(2)}, u32[]{:S(2)}) collective-permute-start(f32[1,8,128]{2,1,0:T(8,128)S(1)} %get-tuple-element.225), channel_id=1, source_target_pairs={{0,4},{4,0},{8,12},{12,8},{16,20},{20,16},{24,28},{28,24},{1,5},{5... | collective-permute-start | bytes 12296 | tf_op jit(solution)/shard_map/ppermute | solution.py:22
  415.1 53.9 %collective-permute-start.51 = (f32[1,8,128]{2,1,0:T(8,128)S(1)}, f32[1,8,128]{2,1,0:T(8,128)S(1)}, u32[]{:S(2)}, u32[]{:S(2)}) collective-permute-start(f32[1,8,128]{2,1,0:T(8,128)S(1)} %get-tuple-element.228), channel_id=1, source_target_pairs={{0,4},{4,0},{8,12},{12,8},{16,20},{20,16},{24,28},{28,24},{1,5},{5... | collective-permute-start | bytes 12296 | tf_op jit(solution)/shard_map/ppermute | solution.py:22
  415.6 53.4 %collective-permute-start.54 = (f32[1,8,128]{2,1,0:T(8,128)S(1)}, f32[1,8,128]{2,1,0:T(8,128)S(1)}, u32[]{:S(2)}, u32[]{:S(2)}) collective-permute-start(f32[1,8,128]{2,1,0:T(8,128)S(1)} %get-tuple-element.227), channel_id=1, source_target_pairs={{0,4},{4,0},{8,12},{12,8},{16,20},{20,16},{24,28},{28,24},{1,5},{5... | collective-permute-start | bytes 12296 | tf_op jit(solution)/shard_map/ppermute | solution.py:22
  415.6 53.3 %collective-permute-start.57 = (f32[1,8,128]{2,1,0:T(8,128)S(1)}, f32[1,8,128]{2,1,0:T(8,128)S(1)}, u32[]{:S(2)}, u32[]{:S(2)}) collective-permute-start(f32[1,8,128]{2,1,0:T(8,128)S(1)} %get-tuple-element.226), channel_id=1, source_target_pairs={{0,4},{4,0},{8,12},{12,8},{16,20},{20,16},{24,28},{28,24},{1,5},{5... | collective-permute-start | bytes 12296 | tf_op jit(solution)/shard_map/ppermute | solution.py:22
  469.0 4.5 collective-permute-start.49
  471.3 4.1 collective-permute-start.52
  471.4 4.2 collective-permute-start.55
  473.4 4.3 collective-permute-start.58
  473.5 4.4 collective-permute-start.50
  475.5 3.8 collective-permute-start.53
  475.7 3.8 collective-permute-start.56
  500.4 4.1 collective-permute-start.61
  502.5 4.2 collective-permute-start.67
  503.0 3.9 collective-permute-start.70
  504.5 4.4 collective-permute-start.62
  504.7 4.2 collective-permute-start.65
  599.0 54.2 %collective-permute-start.72 = (f32[1,8,128]{2,1,0:T(8,128)S(1)}, f32[1,8,128]{2,1,0:T(8,128)S(1)}, u32[]{:S(2)}, u32[]{:S(2)}) collective-permute-start(f32[1,8,128]{2,1,0:T(8,128)S(1)} %get-tuple-element.189), channel_id=1, source_target_pairs={{0,4},{4,0},{8,12},{12,8},{16,20},{20,16},{24,28},{28,24},{1,5},{5... | collective-permute-start | bytes 12296 | tf_op jit(solution)/shard_map/ppermute | solution.py:22
  599.0 54.1 %collective-permute-start.75 = (f32[1,8,128]{2,1,0:T(8,128)S(1)}, f32[1,8,128]{2,1,0:T(8,128)S(1)}, u32[]{:S(2)}, u32[]{:S(2)}) collective-permute-start(f32[1,8,128]{2,1,0:T(8,128)S(1)} %get-tuple-element.192), channel_id=1, source_target_pairs={{0,4},{4,0},{8,12},{12,8},{16,20},{20,16},{24,28},{28,24},{1,5},{5... | collective-permute-start | bytes 12296 | tf_op jit(solution)/shard_map/ppermute | solution.py:22
  599.5 53.7 %collective-permute-start.78 = (f32[1,8,128]{2,1,0:T(8,128)S(1)}, f32[1,8,128]{2,1,0:T(8,128)S(1)}, u32[]{:S(2)}, u32[]{:S(2)}) collective-permute-start(f32[1,8,128]{2,1,0:T(8,128)S(1)} %get-tuple-element.191), channel_id=1, source_target_pairs={{0,4},{4,0},{8,12},{12,8},{16,20},{20,16},{24,28},{28,24},{1,5},{5... | collective-permute-start | bytes 12296 | tf_op jit(solution)/shard_map/ppermute | solution.py:22
  599.6 53.6 %collective-permute-start.81 = (f32[1,8,128]{2,1,0:T(8,128)S(1)}, f32[1,8,128]{2,1,0:T(8,128)S(1)}, u32[]{:S(2)}, u32[]{:S(2)}) collective-permute-start(f32[1,8,128]{2,1,0:T(8,128)S(1)} %get-tuple-element.190), channel_id=1, source_target_pairs={{0,4},{4,0},{8,12},{12,8},{16,20},{20,16},{24,28},{28,24},{1,5},{5... | collective-permute-start | bytes 12296 | tf_op jit(solution)/shard_map/ppermute | solution.py:22
  653.2 4.5 collective-permute-start.73
  655.6 4.1 collective-permute-start.76
  655.7 5.1 collective-permute-start.79
  657.6 4.3 collective-permute-start.82
  657.7 5.3 collective-permute-start.74
  659.7 3.8 collective-permute-start.77
  661.9 3.8 collective-permute-start.83
  684.6 4.1 collective-permute-start.85
  686.7 4.2 collective-permute-start.91
  688.7 4.4 collective-permute-start.86
  690.9 3.8 collective-permute-start.92
  692.0 3.8 collective-permute-start.95
  (38 other events, 1130.8 us)
